TPU v7x, 32 devices: a whole 2x2x4 slice. The times are simulated.
32 devices in a mesh: groups: 1, dp: 32 (over z, y, x, core).
Axes of the slice: x: 2, y: 2, z: 4, core: 2. Of those that a mesh axis runs over, the one named last changes fastest.
Arguments:
- activations: bfloat16 [128, 8192], P(('groups', 'dp')), may hold values from -6 to 6
- cotangent: bfloat16 [128, 8192], P(('groups', 'dp')), may hold values from -6 to 6
- w_gate: bfloat16 [28672, 8192], P('dp'), may hold values from -0.0625 to 0.0625
- w_up: bfloat16 [28672, 8192], P('dp'), may hold values from -0.0625 to 0.0625
- w_down: bfloat16 [28672, 8192], P('dp'), may hold values from -0.03125 to 0.03125
- proj_model: bfloat16 [8192, 192], P('dp'), may hold values from -0.0625 to 0.0625
- proj_hidden: bfloat16 [28672, 192], P('dp'), may hold values from -0.03125 to 0.03125
- seq_ids: int32 [128], P('groups'), may hold values from 0 to 15, never falling along the last dimension, each value on 1 to 16 neighbouring positions
- targets: bfloat16 [256, 3, 64, 64], P(('groups', 'dp')), may hold values from -24 to 24
- target_domain: int32 [256], P(('groups', 'dp')), may hold values from 0 to 31, never falling along the last dimension, each value on 1 to 16 neighbouring positions
Outputs:
- sketches: float32 [16, 3, 64, 64], P('groups')
- scores: float32 [16, 32], P('groups')
Inputs may be any that keep to these rules, and one draw needn't show every extreme that they name: `seq_ids`: never falling along the tokens; each of the 16 sequences has 1 to 16 tokens, one exactly 16. `target_domain`: never falling along the target examples; each of the 32 domains has 1 to 16 examples, one exactly 16.
All inputs are finite; a program needn't handle non-finite values.
Results may differ from a plain program's by a relative error of at most 0.0032.
Values may be sent and summed in bfloat16 or wider, within the bound.
A program may use at most 128 MiB of HBM per device.

v0:
```python
import jax
import jax.numpy as jnp
from jax import lax
from jax.sharding import PartitionSpec as P

DOMAINS = 32
SEQS = 16


def sequence_sketch(vectors, onehot, rank_size):
    blocks = vectors.reshape(vectors.shape[0], 6, rank_size)
    left_side = jnp.stack((blocks[:, 4], blocks[:, 5], blocks[:, 3]), 1)
    right_side = jnp.stack((blocks[:, 0], blocks[:, 1], blocks[:, 2]), 1)
    return jnp.einsum(
        "ns,nka,nkb->skab", onehot, left_side, right_side, precision=lax.Precision.HIGHEST
    )


def on_device(
    activations,
    cotangent,
    w_gate,
    w_up,
    w_down,
    proj_model,
    proj_hidden,
    seq_ids,
    targets,
    target_domain,
):
    rank_size = proj_model.shape[1] // 3
    model_cols = proj_model.shape[0]
    hidden_units = w_gate.shape[0]
    position = lax.axis_index("dp")
    offset = position * model_cols
    rows_in = lax.all_gather(activations, "dp", axis=0, tiled=True)
    gate_value = jnp.einsum("rd,fd->rf", rows_in, w_gate, preferred_element_type=jnp.float32)
    up_value = jnp.einsum("rd,fd->rf", rows_in, w_up, preferred_element_type=jnp.float32)
    columns = lax.dynamic_slice_in_dim(rows_in, offset, model_cols, 1)
    in_model = jnp.dot(columns, proj_model[:, : 2 * rank_size], preferred_element_type=jnp.float32)
    gate_value, up_value, in_model = (gate_value, up_value, in_model)
    forward_all = jnp.concatenate([gate_value, up_value, in_model], 1)
    gate_all = forward_all[:, :hidden_units]
    up_all = forward_all[:, hidden_units : 2 * hidden_units]
    in_model_all = forward_all[:, 2 * hidden_units :]
    gate_value = gate_all
    up_value = up_all
    rows_grad = lax.all_gather(cotangent, "dp", axis=0, tiled=True)
    sigmoid_gate = jax.nn.sigmoid(gate_value)
    silu_gate = gate_value * sigmoid_gate
    hidden = (silu_gate * up_value).astype(jnp.bfloat16)
    grad_hidden = jnp.einsum("rd,fd->rf", rows_grad, w_down, preferred_element_type=jnp.float32)
    grad_gate = (
        grad_hidden * up_value * sigmoid_gate * (1.0 + gate_value * (1.0 - sigmoid_gate))
    ).astype(jnp.bfloat16)
    grad_up = (grad_hidden * silu_gate).astype(jnp.bfloat16)
    columns = lax.dynamic_slice_in_dim(rows_grad, offset, model_cols, 1)
    out_down = jnp.dot(columns, proj_model[:, 2 * rank_size :], preferred_element_type=jnp.float32)
    in_down = jnp.dot(hidden, proj_hidden[:, :rank_size], preferred_element_type=jnp.float32)
    out_gate = jnp.dot(
        grad_gate, proj_hidden[:, rank_size : 2 * rank_size], preferred_element_type=jnp.float32
    )
    out_up = jnp.dot(grad_up, proj_hidden[:, 2 * rank_size :], preferred_element_type=jnp.float32)
    grads_all = jnp.concatenate([out_down, in_down, out_gate, out_up], 1)
    partials = jnp.concatenate([in_model_all, grads_all], 1)
    sequence_range = jnp.arange(SEQS)
    own_vectors = lax.psum_scatter(partials, "dp", scatter_dimension=0, tiled=True)
    own_count = own_vectors.shape[0]
    own_ids = lax.dynamic_slice_in_dim(seq_ids, position * own_count, own_count, 0)
    own_onehot = (own_ids[:, None] == sequence_range[None, :]).astype(jnp.float32)
    local_sketch = sequence_sketch(own_vectors, own_onehot, rank_size)
    sketches = lax.psum(local_sketch, "dp")
    entries = 3 * rank_size * rank_size
    flat_sketch = sketches.reshape(SEQS, entries)
    inverse_norm = lax.rsqrt(jnp.sum(flat_sketch * flat_sketch, 1) + 1e-06)
    domain_onehot = (target_domain[None, :] == jnp.arange(DOMAINS)[:, None]).astype(jnp.bfloat16)
    local_targets = targets.reshape(targets.shape[0], entries)
    domain_count = jnp.sum(domain_onehot.astype(jnp.float32), 1)
    target_products = jnp.dot(
        flat_sketch, local_targets.astype(jnp.float32).T, precision=lax.Precision.HIGHEST
    )
    folded = jnp.dot(
        target_products, domain_onehot.astype(jnp.float32).T, precision=lax.Precision.HIGHEST
    )
    total_scores, total_count = lax.psum((folded, domain_count), "dp")
    scores = total_scores / total_count[None, :] * inverse_norm[:, None]
    return (sketches, scores)


def solution(mesh):
    in_specs = (
        P(("groups", "dp"), None),
        P(("groups", "dp"), None),
        P("dp", None),
        P("dp", None),
        P("dp", None),
        P("dp", None),
        P("dp", None),
        P("groups"),
        P(("groups", "dp"), None, None, None),
        P(("groups", "dp")),
    )
    out_specs = (P("groups", None, None, None), P("groups", None))
    return jax.shard_map(
        on_device, mesh=mesh, in_specs=in_specs, out_specs=out_specs, check_vma=False
    )
```

profile of v0, /device:TPU:0, one launch (start us, length us, event | category | flops | bytes accessed | tf_op | source)
XLA Modules:
  0.0 479.7 jit_solution(16426818172373653184)
XLA Ops:
  7.2 0.0 copy-start
  7.2 0.0 all-gather.5.cloned.1.call-start
  7.2 0.7 all-gather.5.cloned.1.call-update
  7.9 0.0 all-gather.7.cloned.1.call-start
  8.0 0.7 all-gather.7.cloned.1.call-update
  8.7 0.0 all-reduce.7.cloned.1.call-start
  8.7 0.7 dynamic_slice.11
  9.4 0.0 copy-start.3
  9.4 60.4 %all-gather.5.cloned.1.call-done = bf16[32,4,8192]{2,1,0:T(4,128)(2,1)} async-done(((bf16[1,4,8192]{2,1,0:T(4,128)(2,1)}), bf16[32,4,8192]{2,1,0:T(4,128)(2,1)}) %all-gather.5.cloned.1.call-update) | async-done | bytes 2097168 | tf_op jit(solution)/shard_map/all_gather | solution.py:36
  69.8 2.5 reshape.18
  72.3 0.0 copy-done.3
  72.4 0.1 convolution_dynamic-update-slice_fusion
  72.5 55.3 %all-gather.7.cloned.1.call-done = bf16[32,4,8192]{2,1,0:T(4,128)(2,1)} async-done(((bf16[1,4,8192]{2,1,0:T(4,128)(2,1)}), bf16[32,4,8192]{2,1,0:T(4,128)(2,1)}) %all-gather.7.cloned.1.call-update) | async-done | bytes 2097168 | tf_op jit(solution)/shard_map/all_gather | solution.py:48
  127.7 3.9 reshape.20
  131.7 1.0 convolution_dynamic-update-slice_fusion.4
  132.6 10.6 %fusion.30 = f32[128,896]{1,0:T(8,128)S(1)} fusion(bf16[128,8192]{1,0:T(8,128)(2,1)} %reshape.20, bf16[896,8192]{1,0:T(8,128)(2,1)} %param.14), kind=kOutput, calls=%fused_computation.45 | convolution fusion | flops 1879048192 | bytes 17235968 | tf_op jit(solution)/shard_map/rd,fd->rf/dot_general | solution.py:52
  143.2 9.9 %fusion.28 = f32[128,896]{1,0:T(8,128)S(1)} fusion(bf16[128,8192]{1,0:T(8,128)(2,1)S(1)} %reshape.18, bf16[896,8192]{1,0:T(8,128)(2,1)} %param.12), kind=kOutput, calls=%fused_computation.43 | convolution fusion | flops 1879048192 | bytes 17235968 | tf_op jit(solution)/shard_map/rd,fd->rf/dot_general | solution.py:37
  153.1 0.0 copy-start.4
  153.1 9.9 %fusion.29 = f32[128,896]{1,0:T(8,128)S(1)} fusion(bf16[128,8192]{1,0:T(8,128)(2,1)S(1)} %reshape.18, bf16[896,8192]{1,0:T(8,128)(2,1)} %param.13), kind=kOutput, calls=%fused_computation.44 | convolution fusion | flops 1879048192 | bytes 17235968 | tf_op jit(solution)/shard_map/rd,fd->rf/dot_general | solution.py:38
  163.1 0.0 copy-done.4
  163.1 0.3 convolution_dynamic-update-slice_fusion.3
  163.4 0.3 convolution_dynamic-update-slice_fusion.2
  163.7 0.3 convolution_dynamic-update-slice_fusion.1
  164.0 0.0 copy-start.2
  164.0 0.0 copy-start.5
  164.0 0.7 copy-done.2
  164.7 0.0 all-reduce.7.cloned.1.call-update
  164.7 0.2 all-reduce.5.cloned.1.call-start
  165.0 123.5 %all-reduce.7.cloned.1.call-done = f32[128,384]{0,1:T(8,128)} async-done(((f32[128,384]{0,1:T(8,128)}), f32[128,384]{0,1:T(8,128)}) %all-reduce.7.cloned.1.call-update) | async-done | bytes 196624
  288.4 1.0 constant_dynamic-slice_fusion
  289.5 0.1 copy.37
  289.6 0.1 copy.24
  289.7 3.9 convolution_bitcast_fusion
  293.5 0.0 all-reduce.5.cloned.1.call-update
  293.6 0.0 copy-done.5
  293.6 0.1 convert_reduce_fusion
  293.6 134.0 %all-reduce.5.cloned.1.call-done = f32[16,3,64,64]{3,2,0,1:T(8,128)} async-done(((f32[16,3,64,64]{3,2,0,1:T(8,128)}), f32[16,3,64,64]{3,2,0,1:T(8,128)}) %all-reduce.5.cloned.1.call-update) | async-done | bytes 786448 | tf_op jit(solution)/shard_map/psum | solution.py:72
  427.6 0.0 copy-start.1
  427.6 1.8 multiply_reduce_fusion
  429.4 0.0 copy-done
  429.4 0.1 copy-done.1
  429.5 2.3 fusion.2
  431.8 0.2 fusion.21
  432.0 39.2 %all-reduce.1 = (f32[16,32]{1,0:T(8,128)S(1)}, f32[32]{0:T(128)S(1)}) all-reduce(f32[16,32]{1,0:T(8,128)S(1)} %fusion.21, f32[32]{0:T(128)S(1)} %convert_reduce_fusion), channel_id=1, replica_groups=mesh['groups'=1,'dp'=32] {'dp'}, use_global_device_ids=true, to_apply=%region_2.0 | all-reduce | flops 544 | bytes 4352 | tf_op jit(solution)/shard_map/psum | solution.py:85
  471.3 0.7 divide_multiply_fusion
  471.9 1.2 copy.29
  (5 shorter events, 0.0 us)
Async XLA Ops:
  7.2 422.3 %copy-start = (bf16[8,3,64,64]{3,2,1,0:T(8,128)(2,1)S(1)}, bf16[8,3,64,64]{3,2,1,0:T(8,128)(2,1)}, u32[]{:S(2)}) copy-start(bf16[8,3,64,64]{3,2,1,0:T(8,128)(2,1)} %param.18) | copy-start | bytes 589828
  7.2 62.6 %all-gather.5.cloned.1.call-start = ((), (), s32[]{:S(2)}) async-start(), calls=%async_computation.1 | async-start | bytes 2162688 | tf_op jit(solution)/shard_map/all_gather | solution.py:36
  7.9 119.8 %all-gather.7.cloned.1.call-start = ((), (), s32[]{:S(2)}) async-start(), calls=%async_computation.2 | async-start | bytes 2162688 | tf_op jit(solution)/shard_map/all_gather | solution.py:48
  8.7 279.8 %all-reduce.7.cloned.1.call-start = ((), (), s32[]{:S(2)}) async-start(), calls=%async_computation.3 | async-start | bytes 393216
  9.4 62.9 %copy-start.3 = (bf16[256,192]{0,1:T(8,128)(2,1)S(1)}, bf16[256,192]{0,1:T(8,128)(2,1)}, u32[]{:S(2)}) copy-start(bf16[256,192]{0,1:T(8,128)(2,1)} %param.15) | copy-start | bytes 294916
  153.1 10.0 %copy-start.4 = (bf16[896,192]{0,1:T(8,128)(2,1)S(1)}, bf16[896,192]{0,1:T(8,128)(2,1)}, u32[]{:S(2)}) copy-start(bf16[896,192]{0,1:T(8,128)(2,1)} %param.16) | copy-start | bytes 1032196
  164.0 0.7 copy-start.2
  164.0 129.5 %copy-start.5 = (s32[8]{0:T(128)S(1)}, s32[8]{0:T(128)}, u32[]{:S(2)}) copy-start(s32[8]{0:T(128)} %param.19) | copy-start | bytes 100
  164.7 262.9 %all-reduce.5.cloned.1.call-start = ((), (), s32[]{:S(2)}) async-start(), calls=%async_computation | async-start | bytes 3145728 | tf_op jit(solution)/shard_map/psum | solution.py:72
  427.6 1.9 copy-start.1
Sparse Core Ops, SparseCore 0:
  10.8 58.9 all-gather.4
  72.7 55.0 all-gather.6
  164.8 123.5 all-reduce.6
  294.1 133.4 all-reduce.4
where the time goes:
time: 480 us
  waiting for transfers between devices  374 us (78%)
  blocking collectives  39.2 us (8%)
  matrix products  38.8 us (8%)
  between operations  13.9 us (3%)
  local copies, waits for them, and re-layouts  10.4 us (2%)
    psum x1, waiting for transfers between devices, on_device(): sketches = lax.psum(local_sketch, 'dp')  134 us
    unnamed x5, waiting for transfers between devices  125 us
    all_gather x1, waiting for transfers between devices, on_device(): rows_in = lax.all_gather(activations, 'dp', axis=0, tiled=True)  60.4 us
    all_gather x1, waiting for transfers between devices, on_device(): rows_grad = lax.all_gather(cotangent, 'dp', axis=0, tiled=True)  55.3 us
    psum x1, blocking collectives, on_device(): total_scores, total_count = lax.psum((folded, domain_count), 'dp')  39.2 us
    dot_general x1, matrix products, on_device(): jnp.einsum('rd,fd->rf', rows_grad, w_down, preferred_element_type=jnp.flo...  10.6 us
    dot_general x1, matrix products, on_device(): jnp.einsum('rd,fd->rf', rows_in, w_up, preferred_element_type=jnp.float32)  9.95 us
    dot_general x1, matrix products, on_device(): jnp.einsum('rd,fd->rf', rows_in, w_gate, preferred_element_type=jnp.float32)  9.9 us
  transfers between devices with their start and end apart: 4, of which 4 were waited for; matrix products, arithmetic and copies ran while one was open for 1% of the time, Pallas kernels for 0%

commit v1 on v0

--- a/solution.py
+++ b/solution.py
@@ -69,7 +69,9 @@
     own_ids = lax.dynamic_slice_in_dim(seq_ids, position * own_count, own_count, 0)
     own_onehot = (own_ids[:, None] == sequence_range[None, :]).astype(jnp.float32)
     local_sketch = sequence_sketch(own_vectors, own_onehot, rank_size)
-    sketches = lax.psum(local_sketch, "dp")
+    sketches = local_sketch
+    for hop in (1, 2, 4, 8, 16):
+        sketches = sketches + lax.ppermute(sketches, "dp", [(dev, dev ^ hop) for dev in range(32)])
     entries = 3 * rank_size * rank_size
     flat_sketch = sketches.reshape(SEQS, entries)
     inverse_norm = lax.rsqrt(jnp.sum(flat_sketch * flat_sketch, 1) + 1e-06)

time: 480 us -> 524 us (1.092)
  waiting for transfers between devices: 374 us -> 413 us
  starting transfers between devices: 0.34 us -> 8.47 us
    ppermute x0 -> x5, waiting for transfers between devices: none -> 172 us  [on_device(): lax.ppermute(sketches, 'dp', [(dev, dev ^ hop) for dev in range(32)])]
    psum x1 -> x0, waiting for transfers between devices: 134 us -> none  [on_device(): sketches = lax.psum(local_sketch, 'dp')]
    ppermute x0 -> x5, starting transfers between devices: none -> 8.36 us  [on_device(): lax.ppermute(sketches, 'dp', [(dev, dev ^ hop) for dev in range(32)])]
    unnamed x5 -> x4, waiting for transfers between devices: 125 us -> 125 us
  transfers between devices with their start and end apart: 4 -> 8, of which waited for: 4 -> 8; matrix products, arithmetic and copies ran while one was open for 1% -> 1% of each run, Pallas kernels for 0% -> 0%
where the time goes in v1:
time: 524 us
  waiting for transfers between devices  413 us (79%)
  matrix products  37.8 us (7%)
  blocking collectives  37.8 us (7%)
  between operations  13.9 us (3%)
  local copies, waits for them, and re-layouts  10.4 us (2%)
  starting transfers between devices  8.47 us (2%)
    ppermute x5, waiting for transfers between devices, on_device(): lax.ppermute(sketches, 'dp', [(dev, dev ^ hop) for dev in range(32)])  172 us
    unnamed x4, waiting for transfers between devices  125 us
    all_gather x1, waiting for transfers between devices, on_device(): rows_in = lax.all_gather(activations, 'dp', axis=0, tiled=True)  60.4 us
    all_gather x1, waiting for transfers between devices, on_device(): rows_grad = lax.all_gather(cotangent, 'dp', axis=0, tiled=True)  55.3 us
    psum x1, blocking collectives, on_device(): total_scores, total_count = lax.psum((folded, domain_count), 'dp')  37.8 us
    dot_general x1, matrix products, on_device(): jnp.einsum('rd,fd->rf', rows_grad, w_down, preferred_element_type=jnp.flo...  10.6 us
  transfers between devices with their start and end apart: 8, of which 8 were waited for; matrix products, arithmetic and copies ran while one was open for 1% of the time, Pallas kernels for 0%

profile of v1, /device:TPU:0, one launch (start us, length us, event | category | flops | bytes accessed | tf_op | source)
XLA Modules:
  0.0 524.0 jit_solution(16730474176641072675)
XLA Ops:
  7.2 0.0 copy-start
  7.2 0.0 all-gather.5.cloned.1.call-start
  7.2 0.7 all-gather.5.cloned.1.call-update
  7.9 0.0 all-gather.7.cloned.1.call-start
  8.0 0.7 all-gather.7.cloned.1.call-update
  8.7 0.0 all-reduce.4.cloned.1.call-start
  8.7 0.7 dynamic_slice.11
  9.4 60.4 %all-gather.5.cloned.1.call-done = bf16[32,4,8192]{2,1,0:T(4,128)(2,1)} async-done(((bf16[1,4,8192]{2,1,0:T(4,128)(2,1)}), bf16[32,4,8192]{2,1,0:T(4,128)(2,1)}) %all-gather.5.cloned.1.call-update) | async-done | bytes 2097168 | tf_op jit(solution)/shard_map/all_gather | solution.py:36
  69.8 2.5 reshape.18
  72.4 0.1 convolution_dynamic-update-slice_fusion
  72.5 55.3 %all-gather.7.cloned.1.call-done = bf16[32,4,8192]{2,1,0:T(4,128)(2,1)} async-done(((bf16[1,4,8192]{2,1,0:T(4,128)(2,1)}), bf16[32,4,8192]{2,1,0:T(4,128)(2,1)}) %all-gather.7.cloned.1.call-update) | async-done | bytes 2097168 | tf_op jit(solution)/shard_map/all_gather | solution.py:48
  127.7 4.0 reshape.20
  131.7 1.0 convolution_dynamic-update-slice_fusion.4
  132.7 10.6 %fusion.30 = f32[128,896]{1,0:T(8,128)S(1)} fusion(bf16[128,8192]{1,0:T(8,128)(2,1)} %reshape.20, bf16[896,8192]{1,0:T(8,128)(2,1)} %param.14), kind=kOutput, calls=%fused_computation.45 | convolution fusion | flops 1879048192 | bytes 17235968 | tf_op jit(solution)/shard_map/rd,fd->rf/dot_general | solution.py:52
  143.2 9.9 %fusion.28 = f32[128,896]{1,0:T(8,128)S(1)} fusion(bf16[128,8192]{1,0:T(8,128)(2,1)S(1)} %reshape.18, bf16[896,8192]{1,0:T(8,128)(2,1)} %param.12), kind=kOutput, calls=%fused_computation.43 | convolution fusion | flops 1879048192 | bytes 17235968 | tf_op jit(solution)/shard_map/rd,fd->rf/dot_general | solution.py:37
  153.2 9.9 %fusion.29 = f32[128,896]{1,0:T(8,128)S(1)} fusion(bf16[128,8192]{1,0:T(8,128)(2,1)S(1)} %reshape.18, bf16[896,8192]{1,0:T(8,128)(2,1)} %param.13), kind=kOutput, calls=%fused_computation.44 | convolution fusion | flops 1879048192 | bytes 17235968 | tf_op jit(solution)/shard_map/rd,fd->rf/dot_general | solution.py:38
  163.1 0.3 convolution_dynamic-update-slice_fusion.3
  163.4 0.3 convolution_dynamic-update-slice_fusion.2
  163.7 0.3 convolution_dynamic-update-slice_fusion.1
  164.0 0.0 copy-start.1
  164.0 0.7 copy-done.1
  164.7 0.0 all-reduce.4.cloned.1.call-update
  164.7 123.6 %all-reduce.4.cloned.1.call-done = f32[128,384]{0,1:T(8,128)} async-done(((f32[128,384]{0,1:T(8,128)}), f32[128,384]{0,1:T(8,128)}) %all-reduce.4.cloned.1.call-update) | async-done | bytes 196624
  288.4 1.0 constant_dynamic-slice_fusion
  289.5 0.1 copy.37
  289.5 0.1 copy.24
  289.6 2.9 convolution_bitcast_fusion
  292.5 0.1 collective-permute-start
  292.6 3.4 collective-permute-done
  296.0 0.4 add.45
  296.4 1.5 collective-permute-start.1
  297.9 35.0 %collective-permute-done.1 = f32[16,3,64,64]{3,2,0,1:T(8,128)S(1)} collective-permute-done((f32[16,3,64,64]{3,2,0,1:T(8,128)S(1)}, f32[16,3,64,64]{3,2,0,1:T(8,128)S(1)}, u32[]{:S(2)}, u32[]{:S(2)}) %collective-permute-start.1) | collective-permute-done | bytes 786464 | tf_op jit(solution)/shard_map/ppermute | solution.py:74
  332.9 0.4 add.46
  333.2 1.5 collective-permute-start.2
  334.8 34.1 %collective-permute-done.2 = f32[16,3,64,64]{3,2,0,1:T(8,128)S(1)} collective-permute-done((f32[16,3,64,64]{3,2,0,1:T(8,128)S(1)}, f32[16,3,64,64]{3,2,0,1:T(8,128)S(1)}, u32[]{:S(2)}, u32[]{:S(2)}) %collective-permute-start.2) | collective-permute-done | bytes 786464 | tf_op jit(solution)/shard_map/ppermute | solution.py:74
  368.9 0.4 add.47
  369.2 3.4 collective-permute-start.3
  372.7 33.0 %collective-permute-done.3 = f32[16,3,64,64]{3,2,0,1:T(8,128)S(1)} collective-permute-done((f32[16,3,64,64]{3,2,0,1:T(8,128)S(1)}, f32[16,3,64,64]{3,2,0,1:T(8,128)S(1)}, u32[]{:S(2)}, u32[]{:S(2)}) %collective-permute-start.3) | collective-permute-done | bytes 786464 | tf_op jit(solution)/shard_map/ppermute | solution.py:74
  405.6 0.4 add.48
  406.0 1.8 collective-permute-start.4
  407.8 0.1 convert_reduce_fusion
  407.9 66.9 %collective-permute-done.4 = f32[16,3,64,64]{3,2,0,1:T(8,128)S(1)} collective-permute-done((f32[16,3,64,64]{3,2,0,1:T(8,128)S(1)}, f32[16,3,64,64]{3,2,0,1:T(8,128)S(1)}, u32[]{:S(2)}, u32[]{:S(2)}) %collective-permute-start.4) | collective-permute-done | bytes 786464 | tf_op jit(solution)/shard_map/ppermute | solution.py:74
  474.8 0.4 multiply_reduce_fusion
  475.3 1.3 copy.29
  476.5 2.3 fusion.2
  478.8 0.2 fusion.21
  479.1 37.8 %all-reduce.1 = (f32[16,32]{1,0:T(8,128)S(1)}, f32[32]{0:T(128)S(1)}) all-reduce(f32[16,32]{1,0:T(8,128)S(1)} %fusion.21, f32[32]{0:T(128)S(1)} %convert_reduce_fusion), channel_id=1, replica_groups=mesh['groups'=1,'dp'=32] {'dp'}, use_global_device_ids=true, to_apply=%region_1.0 | all-reduce | flops 544 | bytes 4352 | tf_op jit(solution)/shard_map/psum | solution.py:87
  516.8 0.7 divide_multiply_fusion
  (12 shorter events, 0.1 us)
Async XLA Ops:
  7.2 469.4 %copy-start = (bf16[8,3,64,64]{3,2,1,0:T(8,128)(2,1)S(1)}, bf16[8,3,64,64]{3,2,1,0:T(8,128)(2,1)}, u32[]{:S(2)}) copy-start(bf16[8,3,64,64]{3,2,1,0:T(8,128)(2,1)} %param.18) | copy-start | bytes 589828
  7.2 62.6 %all-gather.5.cloned.1.call-start = ((), (), s32[]{:S(2)}) async-start(), calls=%async_computation | async-start | bytes 2162688 | tf_op jit(solution)/shard_map/all_gather | solution.py:36
  7.9 119.8 %all-gather.7.cloned.1.call-start = ((), (), s32[]{:S(2)}) async-start(), calls=%async_computation.1 | async-start | bytes 2162688 | tf_op jit(solution)/shard_map/all_gather | solution.py:48
  8.7 279.7 %all-reduce.4.cloned.1.call-start = ((), (), s32[]{:S(2)}) async-start(), calls=%async_computation.2 | async-start | bytes 393216
  9.4 62.9 %copy-start.2 = (bf16[256,192]{0,1:T(8,128)(2,1)S(1)}, bf16[256,192]{0,1:T(8,128)(2,1)}, u32[]{:S(2)}) copy-start(bf16[256,192]{0,1:T(8,128)(2,1)} %param.15) | copy-start | bytes 294916
  153.2 10.0 %copy-start.3 = (bf16[896,192]{0,1:T(8,128)(2,1)S(1)}, bf16[896,192]{0,1:T(8,128)(2,1)}, u32[]{:S(2)}) copy-start(bf16[896,192]{0,1:T(8,128)(2,1)} %param.16) | copy-start | bytes 1032196
  164.0 0.7 copy-start.1
  292.5 3.5 collective-permute-start
  296.4 36.5 %collective-permute-start.1 = (f32[16,3,64,64]{3,2,0,1:T(8,128)S(1)}, f32[16,3,64,64]{3,2,0,1:T(8,128)S(1)}, u32[]{:S(2)}, u32[]{:S(2)}) collective-permute-start(f32[16,3,64,64]{3,2,0,1:T(8,128)S(1)} %add.45), channel_id=1, source_target_pairs={{0,2},{1,3},{2,0},{3,1},{4,6},{5,7},{6,4},{7,5},{8,10},{9,11},{10,... | collective-permute-start | bytes 2359304 | tf_op jit(solution)/shard_map/ppermute | solution.py:74
  333.2 35.6 %collective-permute-start.2 = (f32[16,3,64,64]{3,2,0,1:T(8,128)S(1)}, f32[16,3,64,64]{3,2,0,1:T(8,128)S(1)}, u32[]{:S(2)}, u32[]{:S(2)}) collective-permute-start(f32[16,3,64,64]{3,2,0,1:T(8,128)S(1)} %add.46), channel_id=1, source_target_pairs={{0,4},{1,5},{2,6},{3,7},{4,0},{5,1},{6,2},{7,3},{8,12},{9,13},{10,... | collective-permute-start | bytes 2359304 | tf_op jit(solution)/shard_map/ppermute | solution.py:74
  369.2 38.6 %copy-start.4 = (s32[8]{0:T(128)S(1)}, s32[8]{0:T(128)}, u32[]{:S(2)}) copy-start(s32[8]{0:T(128)} %param.19) | copy-start | bytes 100
  369.2 36.4 %collective-permute-start.3 = (f32[16,3,64,64]{3,2,0,1:T(8,128)S(1)}, f32[16,3,64,64]{3,2,0,1:T(8,128)S(1)}, u32[]{:S(2)}, u32[]{:S(2)}) collective-permute-start(f32[16,3,64,64]{3,2,0,1:T(8,128)S(1)} %add.47), channel_id=1, source_target_pairs={{0,8},{1,9},{2,10},{3,11},{4,12},{5,13},{6,14},{7,15},{8,0},{9,1},... | collective-permute-start | bytes 2359304 | tf_op jit(solution)/shard_map/ppermute | solution.py:74
  406.0 68.8 %collective-permute-start.4 = (f32[16,3,64,64]{3,2,0,1:T(8,128)S(1)}, f32[16,3,64,64]{3,2,0,1:T(8,128)S(1)}, u32[]{:S(2)}, u32[]{:S(2)}) collective-permute-start(f32[16,3,64,64]{3,2,0,1:T(8,128)S(1)} %add.48), channel_id=1, source_target_pairs={{0,16},{1,17},{2,18},{3,19},{4,20},{5,21},{6,22},{7,23},{8,24},{9,... | collective-permute-start | bytes 2359304 | tf_op jit(solution)/shard_map/ppermute | solution.py:74
Sparse Core Ops, SparseCore 0:
  10.8 58.9 all-gather.4
  72.7 55.0 all-gather.6
  164.8 123.5 all-reduce.3
